TPU v7x, 512 devices: a whole 4x8x8 slice. The times are simulated.
512 devices in a mesh: grp: 32 (over y_lo, z, core), blk: 16 (over x, y_hi).
Axes of the slice: x: 4, y: 8 (y_hi: 4, y_lo: 2; y = y_hi * 2 + y_lo), z: 8, core: 2. Of those that a mesh axis runs over, the one named last changes fastest.
Arguments:
- child_inverse: bfloat16 [32, 2, 2048, 2048], P('grp', None, 'blk'), may hold values from -0.09375 to 0.09375
- border_block: bfloat16 [32, 2, 2048, 2048], P('grp', None, 'blk'), may hold values from -0.09375 to 0.09375
- child_rhs: bfloat16 [32, 2, 2048, 256], P('grp', None, 'blk'), may hold values from -6 to 6
- parent_inverse: bfloat16 [32, 2, 4096, 2048], P('grp', None, 'blk'), may hold values from -0.0625 to 0.0625
- parent_rhs: bfloat16 [32, 2, 2048, 256], P('grp', None, 'blk'), may hold values from -6 to 6
- parent_of: int32 [32, 1], replicated, may hold values from 0 to 15
- owner: int32 [16], replicated, may hold values from 0 to 15, each once
- row_map: int32 [32, 2048], replicated, may hold values from 0 to 4095, as said below
Outputs:
- child_solution: bfloat16 [32, 2, 2048, 256], P('grp', None, 'blk')
- parent_solution: bfloat16 [32, 2, 2048, 256], P('grp', None, 'blk')
Inputs may be any that keep to these rules, and one draw needn't show every extreme that they name: parent_of[c, 0] is the parent front of the sibling front on group c; every parent front has one sibling or more. owner[p] names the pair of groups 2 owner[p] and 2 owner[p] + 1 that holds parent front p; each pair holds one parent. row_map[c, j] differ for different j of one c; border row j with j // 128 = b goes to a parent row h * 2048 + b * 128 + r with h of 0 or 1 and r < 128.
All inputs are finite; a program needn't handle non-finite values.
Results may differ from a plain program's by a relative error of at most 0.008.
Values may be sent and summed in bfloat16 or wider, within the bound.
No kernel may reach another device: no remote copies, remote signals or barrier semaphores. Data moves between devices by JAX's collectives and lax.ppermute only.
A program may use at most 64 MiB of HBM per device.

v0:
```python
import jax
import jax.numpy as jnp
from jax import lax
from jax.sharding import PartitionSpec as P


def swapped(shard, axis, stride):
    return lax.ppermute(shard, axis, [(i, i ^ 1 << stride) for i in range(lax.axis_size(axis))])


def complex_product(left, right):
    real_part = jnp.dot(left[0], right[0], preferred_element_type=jnp.float32) - jnp.dot(
        left[1], right[1], preferred_element_type=jnp.float32
    )
    imag_part = jnp.dot(left[0], right[1], preferred_element_type=jnp.float32) + jnp.dot(
        left[1], right[0], preferred_element_type=jnp.float32
    )
    return jnp.stack([real_part, imag_part])


def column_fold(matrix, shard_piece):
    return complex_product(matrix, shard_piece)


def per_device(
    child_inverse, border_block, child_rhs, parent_inverse, parent_rhs, parent_of, owner, row_map
):
    inverse_rows = child_inverse[0]
    border_rows_block = border_block[0]
    child_solved = column_fold(
        inverse_rows, lax.all_gather(child_rhs[0], "blk", axis=1, tiled=True)
    ).astype(jnp.bfloat16)
    update_rows = (
        -column_fold(border_rows_block, lax.all_gather(child_solved, "blk", axis=1, tiled=True))
    ).astype(jnp.bfloat16)
    group_index = lax.axis_index("grp")
    slot_index = lax.axis_index("blk")
    column_half = group_index % 2
    my_pair = group_index // 2
    border_count = update_rows.shape[1]
    half_rows = parent_rhs.shape[2]
    half_order = parent_inverse.shape[3]
    destination = owner[parent_of[:, 0]]
    local_map = lax.dynamic_slice_in_dim(row_map, slot_index * border_count, border_count, 1)
    row_base = slot_index * half_rows
    offsets = jnp.arange(half_rows, dtype=jnp.int32)
    wanted_rows = column_half * half_order + row_base + offsets
    matches = (local_map[:, None, :] == wanted_rows[None, :, None]) & (destination == my_pair)[
        :, None, None
    ]
    onehot_table = matches.astype(jnp.bfloat16)
    received_sums = jnp.einsum(
        "krj,kcjs->crs",
        onehot_table,
        lax.all_gather(update_rows[None], "grp", axis=0, tiled=True),
        preferred_element_type=jnp.float32,
    )
    right_side = (parent_rhs[0].astype(jnp.float32) + received_sums).astype(jnp.bfloat16)
    parent_block = parent_inverse[0]
    partial_value = column_fold(parent_block, lax.all_gather(right_side, "blk", axis=1, tiled=True))
    partner_part = swapped(partial_value.astype(jnp.bfloat16), "grp", 0).astype(partial_value.dtype)
    combined = partial_value + partner_part
    own_rows = lax.dynamic_slice_in_dim(combined, column_half * half_rows, half_rows, 1)
    return (child_solved[None], own_rows.astype(jnp.bfloat16)[None])


def solution(mesh):
    in_specs = (
        P("grp", None, "blk", None),
        P("grp", None, "blk", None),
        P("grp", None, "blk", None),
        P("grp", None, "blk", None),
        P("grp", None, "blk", None),
        P(),
        P(),
        P(),
    )
    out_specs = (P("grp", None, "blk", None), P("grp", None, "blk", None))
    return jax.shard_map(
        per_device, mesh=mesh, in_specs=in_specs, out_specs=out_specs, check_vma=False
    )
```

profile of v0, /device:TPU:1, one launch (start us, length us, event | category | flops | bytes accessed | tf_op | source)
XLA Modules:
  0.0 306.5 jit_solution(10172488542410082918)
XLA Ops:
  7.2 0.0 all-gather.12.cloned.1.call-start
  7.2 0.7 all-gather.12.cloned.1.call-update
  7.9 0.0 all-gather.6.cloned.1.call-start
  8.0 72.5 %all-gather.12.cloned.1.call-done = bf16[1,2,2048,256]{3,2,1,0:T(8,128)(2,1)} async-done(((bf16[1,2,128,256]{3,2,1,0:T(8,128)(2,1)}), bf16[1,2,2048,256]{3,2,1,0:T(8,128)(2,1)}) %all-gather.12.cloned.1.call-update) | async-done | bytes 2097168 | tf_op jit(solution)/shard_map/all_gather | solution.py:31
  80.5 1.8 fusion.28
  82.3 1.5 fusion.29
  83.9 0.3 fusion.17
  84.2 0.3 fusion.18
  84.5 0.7 pad_maximum_fusion.2
  85.2 0.0 all-gather.8.cloned.1.call-start
  85.3 62.4 %all-gather.6.cloned.1.call-done = bf16[2,2048,256]{2,1,0:T(8,128)(2,1)} async-done(((bf16[2,128,256]{2,1,0:T(8,128)(2,1)}), bf16[2,2048,256]{2,1,0:T(8,128)(2,1)}) %all-gather.6.cloned.1.call-update) | async-done | bytes 2097168 | tf_op jit(solution)/shard_map/all_gather | solution.py:34
  147.6 1.8 fusion.30
  149.5 0.1 copy-done.4
  149.5 0.5 fusion.31
  150.0 0.5 fusion.16
  150.5 0.5 fusion.15
  151.0 0.8 copy.17
  151.8 0.0 all-gather.10.cloned.1.call-start
  151.9 0.1 copy.16
  152.1 0.7 gather_fusion
  152.8 67.6 %all-gather.8.cloned.1.call-done = bf16[32,2,128,256]{3,2,1,0:T(8,128)(2,1)} async-done(((bf16[1,2,128,256]{3,2,1,0:T(8,128)(2,1)}), bf16[32,2,128,256]{3,2,1,0:T(8,128)(2,1)}) %all-gather.8.cloned.1.call-update) | async-done | bytes 4194320 | tf_op jit(solution)/shard_map/all_gather | solution.py:55
  220.4 4.3 %fusion.12 = bf16[2,128,256]{1,2,0:T(8,128)(2,1)} fusion(bf16[32,2,128,256]{3,2,1,0:T(8,128)(2,1)} %all-gather.8.cloned.1.call-done, s32[32,128]{1,0:T(8,128)S(1)} %constant_dynamic-slice_fusion, s32[128]{0:T(128)S(1)} %iota_add_fusion, pred[32]{0:T(512)(128)(4,1)S(1)} %broadcast_compare_fusion, bf16[1,2,128,256]{2,3,1,0:T(8,128)(2,1)S(1)} %copy.16), kind=kOutput, calls=%fused_computation.11 | convolution fusion | flops 538116096 | bytes 4473376 | tf_op jit(solution)/shard_map/krj,kcjs->crs/dot_general | solution.py:52
  224.7 64.1 %all-gather.10.cloned.1.call-done = bf16[2,2048,256]{1,2,0:T(8,128)(2,1)} async-done(((bf16[2,128,256]{1,2,0:T(8,128)(2,1)}), bf16[2,2048,256]{1,2,0:T(8,128)(2,1)}) %all-gather.10.cloned.1.call-update) | async-done | bytes 2097168 | tf_op jit(solution)/shard_map/all_gather | solution.py:60
  288.8 1.8 fusion.23
  290.7 0.1 copy-done.6
  290.7 0.5 fusion.21
  291.2 0.5 fusion.8
  291.7 0.5 fusion.7
  292.2 5.8 %collective-permute-start = (bf16[2,256,256]{1,2,0:T(8,128)(2,1)S(1)}, bf16[2,256,256]{1,2,0:T(8,128)(2,1)S(1)}, u32[]{:S(2)}, u32[]{:S(2)}) collective-permute-start(bf16[2,256,256]{1,2,0:T(8,128)(2,1)S(1)} %fusion.36), channel_id=1, source_target_pairs={{0,16},{16,0},{32,48},{48,32},{64,80},{80,64},{96,112},{112,96},{1... | collective-permute-start | bytes 786440 | tf_op jit(solution)/shard_map/ppermute | solution.py:8
  298.0 0.7 pad_maximum_fusion.1
  298.7 0.5 collective-permute-done
  299.2 0.8 copy.19
  (29 shorter events, 0.2 us)
Async XLA Ops:
  7.2 145.6 %copy-start = (s32[32,2048]{1,0:T(8,128)S(1)}, s32[32,2048]{1,0:T(8,128)}, u32[]{:S(2)}) copy-start(s32[32,2048]{1,0:T(8,128)} %param.15) | copy-start | bytes 786436
  7.2 75.1 %copy-start.7 = (bf16[1,2,128,2048]{3,2,1,0:T(8,128)(2,1)S(1)}, bf16[1,2,128,2048]{3,2,1,0:T(8,128)(2,1)}, u32[]{:S(2)}) copy-start(bf16[1,2,128,2048]{3,2,1,0:T(8,128)(2,1)} %param.8) | copy-start | bytes 3145732
  7.2 73.3 %all-gather.12.cloned.1.call-start = ((), (), s32[]{:S(2)}) async-start(), calls=%async_computation.3 | async-start | bytes 2228224 | tf_op jit(solution)/shard_map/all_gather | solution.py:31
  7.9 139.7 %all-gather.6.cloned.1.call-start = ((), (), s32[]{:S(2)}) async-start(), calls=%async_computation | async-start | bytes 2228224 | tf_op jit(solution)/shard_map/all_gather | solution.py:34
  80.5 3.4 %copy-start.5 = (bf16[1,2,2048,256]{3,2,1,0:T(8,128)(2,1)S(1)}, bf16[1,2,2048,256]{3,2,1,0:T(8,128)(2,1)}, u32[]{:S(2)}) copy-start(bf16[1,2,2048,256]{3,2,1,0:T(8,128)(2,1)} %all-gather.12.cloned.1.call-done) | copy-start | bytes 6291460
  83.9 63.8 %copy-start.8 = (bf16[1,2,128,2048]{3,2,1,0:T(8,128)(2,1)S(1)}, bf16[1,2,128,2048]{3,2,1,0:T(8,128)(2,1)}, u32[]{:S(2)}) copy-start(bf16[1,2,128,2048]{3,2,1,0:T(8,128)(2,1)} %param.9) | copy-start | bytes 3145732
  85.2 135.2 %all-gather.8.cloned.1.call-start = ((), (), s32[]{:S(2)}) async-start(), calls=%async_computation.1 | async-start | bytes 4325376 | tf_op jit(solution)/shard_map/all_gather | solution.py:55
  147.6 1.9 copy-start.4
  150.5 1.4 copy-start.2
  150.5 1.6 copy-start.9
  150.5 1.6 copy-start.1
  151.8 137.0 %all-gather.10.cloned.1.call-start = ((), (), s32[]{:S(2)}) async-start(), calls=%async_computation.2 | async-start | bytes 2228224 | tf_op jit(solution)/shard_map/all_gather | solution.py:60
  152.8 136.0 %copy-start.3 = (bf16[1,2,256,2048]{3,2,1,0:T(8,128)(2,1)S(1)}, bf16[1,2,256,2048]{3,2,1,0:T(8,128)(2,1)}, u32[]{:S(2)}) copy-start(bf16[1,2,256,2048]{3,2,1,0:T(8,128)(2,1)} %param.11) | copy-start | bytes 6291460
  288.8 1.9 copy-start.6
  292.2 6.9 %collective-permute-start = (bf16[2,256,256]{1,2,0:T(8,128)(2,1)S(1)}, bf16[2,256,256]{1,2,0:T(8,128)(2,1)S(1)}, u32[]{:S(2)}, u32[]{:S(2)}) collective-permute-start(bf16[2,256,256]{1,2,0:T(8,128)(2,1)S(1)} %fusion.36), channel_id=1, source_target_pairs={{0,16},{16,0},{32,48},{48,32},{64,80},{80,64},{96,112},{112,96},{1... | collective-permute-start | bytes 786440 | tf_op jit(solution)/shard_map/ppermute | solution.py:8
Sparse Core Ops, SparseCore 0:
  11.1 69.3 all-gather.11
  85.3 62.2 all-gather.5
  151.9 68.4 all-gather.7
  224.8 63.9 all-gather.9
where the time goes:
time: 307 us; the launch traced here: 306 us
  waiting for transfers between devices  268 us (87%)
  matrix products  14.8 us (5%)
  between operations  14.1 us (5%)
  starting transfers between devices  5.96 us (2%)
    all_gather x1, waiting for transfers between devices, per_device(): lax.all_gather(child_rhs[0], 'blk', axis=1, tiled=True)  72.5 us
    all_gather x1, waiting for transfers between devices, per_device(): lax.all_gather(update_rows[None], 'grp', axis=0, tiled=True)  67.6 us
    all_gather x1, waiting for transfers between devices, per_device(): lax.all_gather(right_side, 'blk', axis=1, tiled=True)  64.1 us
    all_gather x1, waiting for transfers between devices, per_device(): lax.all_gather(child_solved, 'blk', axis=1, tiled=True)  62.4 us
  transfers between devices with their start and end apart: 5, of which 5 were waited for; matrix products, arithmetic and copies ran while one was open for 0% of the time, Pallas kernels for 0%

commit v1 on v0

--- a/solution.py
+++ b/solution.py
@@ -28,7 +28,10 @@
     inverse_rows = child_inverse[0]
     border_rows_block = border_block[0]
     child_solved = column_fold(
-        inverse_rows, lax.all_gather(child_rhs[0], "blk", axis=1, tiled=True)
+        inverse_rows,
+        jnp.concatenate(
+            lax.all_to_all(jnp.stack([child_rhs[0]] * lax.axis_size("blk")), "blk", 0, 0), axis=1
+        ),
     ).astype(jnp.bfloat16)
     update_rows = (
         -column_fold(border_rows_block, lax.all_gather(child_solved, "blk", axis=1, tiled=True))

time: 307 us -> 296 us (0.964)
  waiting for transfers between devices: 268 us -> 196 us
  blocking collectives: 0 us -> 61 us
    all_gather x1 -> x0, waiting for transfers between devices: 72.5 us -> none  [per_device(): lax.all_gather(child_rhs[0], 'blk', axis=1, tiled=True)]
    all_to_all x0 -> x1, blocking collectives: none -> 61 us  [per_device(): lax.all_to_all(jnp.stack([child_rhs[0]] * lax.axis_size('blk')), 'blk', 0...]
  transfers between devices with their start and end apart: 5 -> 4, of which waited for: 5 -> 4; matrix products, arithmetic and copies ran while one was open for 0% -> 1% of each run, Pallas kernels for 0% -> 0%
where the time goes in v1:
time: 296 us; the launch traced here: 295 us
  waiting for transfers between devices  196 us (66%)
  blocking collectives  61 us (21%)
  between operations  14 us (5%)
  matrix products  12 us (4%)
  starting transfers between devices  5.93 us (2%)
  local copies, waits for them, and re-layouts  4.91 us (2%)
    all_gather x1, waiting for transfers between devices, per_device(): lax.all_gather(update_rows[None], 'grp', axis=0, tiled=True)  67.6 us
    all_gather x1, waiting for transfers between devices, per_device(): lax.all_gather(right_side, 'blk', axis=1, tiled=True)  64.1 us
    all_gather x1, waiting for transfers between devices, per_device(): lax.all_gather(child_solved, 'blk', axis=1, tiled=True)  63.9 us
    all_to_all x1, blocking collectives, per_device(): lax.all_to_all(jnp.stack([child_rhs[0]] * lax.axis_size('blk')), 'blk', 0...  61 us
  transfers between devices with their start and end apart: 4, of which 4 were waited for; matrix products, arithmetic and copies ran while one was open for 1% of the time, Pallas kernels for 0%

profile of v1, /device:TPU:1, one launch (start us, length us, event | category | flops | bytes accessed | tf_op | source)
XLA Modules:
  0.0 295.4 jit_solution(4751731415797952556)
XLA Ops:
  7.2 1.2 stack.39
  8.4 61.0 %all_to_all.5 = bf16[16,2,128,256]{3,2,1,0:T(8,128)(2,1)S(1)} all-to-all(bf16[16,2,128,256]{3,2,1,0:T(8,128)(2,1)S(1)} %stack.39), channel_id=1, replica_groups=mesh['grp'=32,'blk'=16] {'blk'}, dimensions={0} | all-to-all | bytes 4194304 | tf_op jit(solution)/shard_map/all_to_all | solution.py:33
  69.4 0.2 fusion.59
  69.6 1.0 copy-done.2
  70.7 0.3 fusion.43
  71.0 0.3 fusion.41
  71.3 0.3 fusion.17
  71.6 0.3 fusion.18
  71.9 0.7 pad_maximum_fusion.2
  72.6 0.0 all-gather.6.cloned.1.call-start
  72.7 63.9 %all-gather.4.cloned.1.call-done = bf16[2,2048,256]{2,1,0:T(8,128)(2,1)} async-done(((bf16[2,128,256]{2,1,0:T(8,128)(2,1)}), bf16[2,2048,256]{2,1,0:T(8,128)(2,1)}) %all-gather.4.cloned.1.call-update) | async-done | bytes 2097168 | tf_op jit(solution)/shard_map/all_gather | solution.py:37
  136.6 1.8 fusion.28
  138.4 0.1 copy-done.5
  138.5 0.5 fusion.29
  138.9 0.5 fusion.16
  139.5 0.5 fusion.15
  140.0 0.8 copy.17
  140.8 0.0 all-gather.8.cloned.1.call-start
  140.8 0.1 copy.16
  141.0 0.7 gather_fusion
  141.8 67.6 %all-gather.6.cloned.1.call-done = bf16[32,2,128,256]{3,2,1,0:T(8,128)(2,1)} async-done(((bf16[1,2,128,256]{3,2,1,0:T(8,128)(2,1)}), bf16[32,2,128,256]{3,2,1,0:T(8,128)(2,1)}) %all-gather.6.cloned.1.call-update) | async-done | bytes 4194320 | tf_op jit(solution)/shard_map/all_gather | solution.py:58
  209.3 4.3 %fusion.12 = bf16[2,128,256]{1,2,0:T(8,128)(2,1)} fusion(bf16[32,2,128,256]{3,2,1,0:T(8,128)(2,1)} %all-gather.6.cloned.1.call-done, s32[32,128]{1,0:T(8,128)S(1)} %constant_dynamic-slice_fusion, s32[128]{0:T(128)S(1)} %iota_add_fusion, pred[32]{0:T(512)(128)(4,1)S(1)} %broadcast_compare_fusion, bf16[1,2,128,256]{2,3,1,0:T(8,128)(2,1)S(1)} %copy.16), kind=kOutput, calls=%fused_computation.11 | convolution fusion | flops 538116096 | bytes 4473376 | tf_op jit(solution)/shard_map/krj,kcjs->crs/dot_general | solution.py:55
  213.6 64.1 %all-gather.8.cloned.1.call-done = bf16[2,2048,256]{1,2,0:T(8,128)(2,1)} async-done(((bf16[2,128,256]{1,2,0:T(8,128)(2,1)}), bf16[2,2048,256]{1,2,0:T(8,128)(2,1)}) %all-gather.8.cloned.1.call-update) | async-done | bytes 2097168 | tf_op jit(solution)/shard_map/all_gather | solution.py:63
  277.7 1.8 fusion.23
  279.6 0.1 copy-done.6
  279.7 0.5 fusion.21
  280.1 0.5 fusion.8
  280.6 0.5 fusion.7
  281.1 5.8 %collective-permute-start = (bf16[2,256,256]{1,2,0:T(8,128)(2,1)S(1)}, bf16[2,256,256]{1,2,0:T(8,128)(2,1)S(1)}, u32[]{:S(2)}, u32[]{:S(2)}) collective-permute-start(bf16[2,256,256]{1,2,0:T(8,128)(2,1)S(1)} %fusion.34), channel_id=1, source_target_pairs={{0,16},{16,0},{32,48},{48,32},{64,80},{80,64},{96,112},{112,96},{1... | collective-permute-start | bytes 786440 | tf_op jit(solution)/shard_map/ppermute | solution.py:8
  286.9 0.7 pad_maximum_fusion.1
  287.6 0.5 collective-permute-done
  288.1 0.8 copy.19
  (27 shorter events, 0.3 us)
Async XLA Ops:
  7.2 134.6 %copy-start = (s32[32,2048]{1,0:T(8,128)S(1)}, s32[32,2048]{1,0:T(8,128)}, u32[]{:S(2)}) copy-start(s32[32,2048]{1,0:T(8,128)} %param.15) | copy-start | bytes 786436
  7.2 129.4 %all-gather.4.cloned.1.call-start = ((), (), s32[]{:S(2)}) async-start(), calls=%async_computation.1 | async-start | bytes 2228224 | tf_op jit(solution)/shard_map/all_gather | solution.py:37
  69.4 1.2 copy-start.2
  71.3 65.3 %copy-start.7 = (bf16[1,2,128,2048]{3,2,1,0:T(8,128)(2,1)S(1)}, bf16[1,2,128,2048]{3,2,1,0:T(8,128)(2,1)}, u32[]{:S(2)}) copy-start(bf16[1,2,128,2048]{3,2,1,0:T(8,128)(2,1)} %param.9) | copy-start | bytes 3145732
  72.6 136.7 %all-gather.6.cloned.1.call-start = ((), (), s32[]{:S(2)}) async-start(), calls=%async_computation.2 | async-start | bytes 4325376 | tf_op jit(solution)/shard_map/all_gather | solution.py:58
  136.6 1.9 copy-start.5
  139.4 1.4 copy-start.3
  139.4 1.6 copy-start.8
  139.4 1.6 copy-start.1
  140.8 137.0 %all-gather.8.cloned.1.call-start = ((), (), s32[]{:S(2)}) async-start(), calls=%async_computation.3 | async-start | bytes 2228224 | tf_op jit(solution)/shard_map/all_gather | solution.py:63
  141.8 136.0 %copy-start.4 = (bf16[1,2,256,2048]{3,2,1,0:T(8,128)(2,1)S(1)}, bf16[1,2,256,2048]{3,2,1,0:T(8,128)(2,1)}, u32[]{:S(2)}) copy-start(bf16[1,2,256,2048]{3,2,1,0:T(8,128)(2,1)} %param.11) | copy-start | bytes 6291460
  277.7 1.9 copy-start.6
  281.1 7.0 %collective-permute-start = (bf16[2,256,256]{1,2,0:T(8,128)(2,1)S(1)}, bf16[2,256,256]{1,2,0:T(8,128)(2,1)S(1)}, u32[]{:S(2)}, u32[]{:S(2)}) collective-permute-start(bf16[2,256,256]{1,2,0:T(8,128)(2,1)S(1)} %fusion.34), channel_id=1, source_target_pairs={{0,16},{16,0},{32,48},{48,32},{64,80},{80,64},{96,112},{112,96},{1... | collective-permute-start | bytes 786440 | tf_op jit(solution)/shard_map/ppermute | solution.py:8
Sparse Core Ops, SparseCore 0:
  72.8 63.7 all-gather.3
  140.9 68.4 all-gather.5
  213.8 63.9 all-gather.7
